TPU v7x, 128 devices: a whole 4x4x4 slice. The times are simulated.
128 devices in a mesh: req: 32 (over x, z, core), tp: 4 (over y).
Axes of the slice: x: 4, y: 4, z: 4, core: 2. Of those that a mesh axis runs over, the one named last changes fastest.
Arguments:
- hidden_states: bfloat16 [8192, 2048], P('req'), may hold values from -30 to 30
- norm_gain: float32 [2048], replicated, may hold values from 0.5 to 1.5
- head: bfloat16 [2048, 98304], P(None, ('req', 'tp')), may hold values from -1 to 1
- target_ids: int32 [8192], P('req'), may hold values from 0 to 98303
- lengths: int32 [32], P('req'), may hold values from 32 to 256, as said below
Outputs:
- token_logprob: float32 [8192], P('req')
- token_entropy: float32 [8192], P('req')
- seq_mean_logprob: float32 [32], P('req')
- seq_top_logit: float32 [32], P('req')
Inputs may be any that keep to these rules, and one draw needn't show every extreme that they name: `lengths`: each completion has at least 32 and at most 256 live slots; some completion has exactly 256.
All inputs are finite; a program needn't handle non-finite values.
Results may differ from a plain program's by a relative error of at most 0.0018.
Values may be sent and summed in bfloat16 or wider, within the bound.
A program may use at most 128 MiB of HBM per device.

v0:
```python
import jax
import jax.numpy as jnp
from jax import lax
from jax.sharding import PartitionSpec as P

CHUNKS = 4


def chunk_stats(block, target, matrix, vocab_ids):
    logits = jnp.dot(block, matrix, preferred_element_type=jnp.float32)
    top = jnp.max(logits, axis=-1)
    shifted = jnp.exp(logits - top[:, None])
    weight_sum = jnp.sum(shifted, axis=-1)
    weighted = jnp.sum(shifted * logits, axis=-1)
    hit = vocab_ids == target[:, None]
    picked = jnp.sum(jnp.where(hit, logits, 0.0), axis=-1)
    return jnp.stack([top, weight_sum, weighted, picked])


def merge(stats, axis):
    top = jnp.max(stats[:, 0], axis=axis)
    factor = jnp.exp(stats[:, 0] - jnp.expand_dims(top, axis))
    return (
        top,
        jnp.sum(stats[:, 1] * factor, axis=axis),
        jnp.sum(stats[:, 2] * factor, axis=axis),
        jnp.sum(stats[:, 3], axis=axis),
    )


def per_device(hidden_states, norm_gain, head, target_ids, lengths):
    feats = hidden_states.astype(jnp.float32)
    scale = lax.rsqrt(jnp.mean(feats * feats, axis=-1, keepdims=True) + 1e-06)
    normed = (feats * scale * norm_gain).astype(jnp.bfloat16)
    rows = hidden_states.shape[0]
    vdev = head.shape[1]
    n_req = lax.axis_size("req")
    n_tp = lax.axis_size("tp")
    vbase = (lax.axis_index("req") * n_tp + lax.axis_index("tp")) * vdev
    own_vocab = lax.broadcasted_iota(jnp.int32, (1, vdev), 1) + vbase
    step = rows // CHUNKS
    digits = jnp.concatenate([target_ids % 64, target_ids // 64 % 64, target_ids // 4096])
    extra = jnp.zeros((16, normed.shape[1]), jnp.bfloat16)
    extra = extra.at[0, : 3 * rows].set(digits.astype(jnp.bfloat16))
    parts = []
    targets = None
    for c in range(CHUNKS):
        piece = normed[c * step : (c + 1) * step]
        if c == 0:
            piece = jnp.concatenate([piece, extra], axis=0)
        block = lax.all_gather(piece, "req", axis=0, tiled=False)
        if c == 0:
            code = block[:, step, : 3 * rows].astype(jnp.int32).reshape(n_req, 3, rows)
            targets = code[:, 0] + code[:, 1] * 64 + code[:, 2] * 4096
            block = block[:, :step]
        target = targets[:, c * step : (c + 1) * step].reshape(-1)
        st = chunk_stats(block.reshape(-1, block.shape[2]), target, head, own_vocab)
        parts.append(st.reshape(4, n_req, step))
    stats = jnp.concatenate(parts, axis=2)
    arrived = lax.all_to_all(stats, "req", split_axis=1, concat_axis=1, tiled=True)
    own = merge(jnp.moveaxis(arrived, 1, 0), axis=0)
    own = jnp.stack(own)
    everyone = lax.all_gather(own, "tp", axis=0)
    top, weight_sum, weighted, picked = merge(everyone, axis=0)
    log_norm = top + jnp.log(weight_sum)
    live = jnp.arange(rows, dtype=jnp.int32) < lengths[0]
    logprob = jnp.where(live, picked - log_norm, jnp.float32(0.0))
    entropy = jnp.where(live, log_norm - weighted / weight_sum, jnp.float32(0.0))
    mean_lp = (jnp.sum(logprob) / lengths[0].astype(jnp.float32)).reshape(1)
    top_live = jnp.max(jnp.where(live, top, jnp.float32(-1e30))).reshape(1)
    return (logprob, entropy, mean_lp, top_live)


def solution(mesh):
    in_specs = (P("req", None), P(), P(None, ("req", "tp")), P("req"), P("req"))
    out_specs = (P("req"), P("req"), P("req"), P("req"))
    return jax.shard_map(
        per_device, mesh=mesh, in_specs=in_specs, out_specs=out_specs, check_vma=False
    )
```

profile of v0, /device:TPU:0, one launch (start us, length us, event | category | flops | bytes accessed | tf_op | source)
XLA Modules:
  0.0 306.7 jit_solution(13360459740497236305)
XLA Ops:
  7.2 1.7 fusion.4
  8.9 1.5 fusion.6
  10.4 0.9 fusion.33
  11.4 0.7 all-gather.15.cloned.1.call-update
  12.2 0.7 all-gather.17.cloned.1.call-update
  12.9 0.7 fusion.29
  13.7 0.8 pad_maximum_fusion
  14.5 52.5 %all-gather.13.cloned.1.call-done = bf16[2048,2048]{1,0:T(8,128)(2,1)} async-done(((bf16[64,2048]{1,0:T(8,128)(2,1)}), bf16[2048,2048]{1,0:T(8,128)(2,1)}) %all-gather.13.cloned.1.call-update) | async-done | bytes 8388624 | tf_op jit(solution)/shard_map/all_gather | solution.py:51
  67.0 10.8 %fusion.38 = (f32[2048]{0:T(1024)S(1)}, f32[2048,768]{0,1:T(8,128)}) fusion(bf16[2048,2048]{1,0:T(8,128)(2,1)} %all-gather.13.cloned.1.call-done, bf16[2048,768]{1,0:T(8,128)(2,1)S(1)} %copy-done), kind=kOutput, calls=%fused_computation.92 | convolution fusion | flops 6444021760 | bytes 17833984 | tf_op jit(solution)/shard_map/dot_general | solution.py:10
  77.8 0.1 stack.80
  77.9 43.9 %all-gather.15.cloned.1.call-done = bf16[2048,2048]{1,0:T(8,128)(2,1)} async-done(((bf16[64,2048]{1,0:T(8,128)(2,1)}), bf16[2048,2048]{1,0:T(8,128)(2,1)}) %all-gather.15.cloned.1.call-update) | async-done | bytes 8388624 | tf_op jit(solution)/shard_map/all_gather | solution.py:51
  121.8 10.8 %fusion.39 = (f32[2048]{0:T(1024)S(1)}, f32[2048,768]{0,1:T(8,128)}) fusion(bf16[2048,2048]{1,0:T(8,128)(2,1)} %all-gather.15.cloned.1.call-done, bf16[2048,768]{1,0:T(8,128)(2,1)S(1)} %copy-done), kind=kOutput, calls=%fused_computation.93 | convolution fusion | flops 6444021760 | bytes 17833984 | tf_op jit(solution)/shard_map/dot_general | solution.py:10
  132.6 0.1 stack.85
  132.7 44.0 %all-gather.17.cloned.1.call-done = bf16[2048,2048]{1,0:T(8,128)(2,1)} async-done(((bf16[64,2048]{1,0:T(8,128)(2,1)}), bf16[2048,2048]{1,0:T(8,128)(2,1)}) %all-gather.17.cloned.1.call-update) | async-done | bytes 8388624 | tf_op jit(solution)/shard_map/all_gather | solution.py:51
  176.7 10.8 %fusion.40 = (f32[2048]{0:T(1024)S(1)}, f32[2048,768]{0,1:T(8,128)}) fusion(bf16[2048,2048]{1,0:T(8,128)(2,1)} %all-gather.17.cloned.1.call-done, bf16[2048,768]{1,0:T(8,128)(2,1)S(1)} %copy-done), kind=kOutput, calls=%fused_computation.94 | convolution fusion | flops 6444021760 | bytes 17833984 | tf_op jit(solution)/shard_map/dot_general | solution.py:10
  187.4 0.1 stack.90
  187.5 48.7 %all-gather.11.cloned.1.call-done = bf16[2560,2048]{1,0:T(8,128)(2,1)} async-done(((bf16[80,2048]{1,0:T(8,128)(2,1)}), bf16[2560,2048]{1,0:T(8,128)(2,1)}) %all-gather.11.cloned.1.call-update) | async-done | bytes 10485776 | tf_op jit(solution)/shard_map/all_gather | solution.py:51
  236.2 1.0 slice.104
  237.3 8.4 %slice.103 = bf16[32,64,2048]{2,1,0:T(8,128)(2,1)} slice(bf16[32,80,2048]{2,1,0:T(8,128)(2,1)} %bitcast.69), slice={[0:32], [0:64], [0:2048]} | slice | bytes 16777216 | tf_op jit(solution)/shard_map/slice | solution.py:55
  246.2 10.9 %fusion.37 = (f32[2048]{0:T(1024)S(1)}, f32[2048,768]{0,1:T(8,128)}) fusion(bf16[2048,2048]{1,0:T(8,128)(2,1)} %bitcast.67, bf16[2048,768]{1,0:T(8,128)(2,1)S(1)} %copy-done), kind=kOutput, calls=%fused_computation.91 | convolution fusion | flops 6444021760 | bytes 17833984 | tf_op jit(solution)/shard_map/dot_general | solution.py:10
  257.1 0.1 stack.75
  257.2 12.0 %fusion.3 = (f32[2048]{0:T(1024)S(1)}, f32[2048]{0:T(1024)S(1)}, f32[2048]{0:T(1024)S(1)}, f32[2048]{0:T(1024)S(1)}, f32[2048]{0:T(1024)S(1)}, /*index=5*/f32[20...) fusion(f32[2048,768]{0,1:T(8,128)} %get-tuple-element.71, ...), kind=kLoop, calls=%fused_computation.15 | loop fusion | flops 44015616 | bytes 25332736 | tf_op jit(solution)/shard_map/reduce_sum | solution.py:13
  269.2 0.1 stack.76
  269.5 0.1 stack.82
  269.7 0.1 stack.87
  270.0 0.1 stack.92
  270.1 1.1 maximum_maximum_fusion
  271.3 5.4 %all-to-all-start = ((f32[4,32,256]{2,0,1:T(4,128)}), f32[4,32,256]{2,0,1:T(4,128)S(1)}, u32[]{:S(2)}, u32[]{:S(2)}) async-start(f32[4,32,256]{2,0,1:T(4,128)} %maximum_maximum_fusion), calls=%async_computation | async-start | bytes 262144 | tf_op jit(solution)/shard_map/all_to_all | solution.py:60
  277.4 7.2 %all-to-all-done = f32[4,32,256]{2,0,1:T(4,128)S(1)} async-done(((f32[4,32,256]{2,0,1:T(4,128)}), f32[4,32,256]{2,0,1:T(4,128)S(1)}, u32[]{:S(2)}, u32[]{:S(2)}) %all-to-all-start) | async-done | bytes 131104 | tf_op jit(solution)/shard_map/all_to_all | solution.py:60
  284.6 0.1 fusion.34
  284.7 12.3 %all-gather.5 = f32[4,4,256]{2,1,0:T(4,128)S(1)} all-gather(f32[1,4,256]{2,1,0:T(4,128)S(1)} %maximum_bitcast_fusion), channel_id=6, replica_groups=mesh['req'=32,'tp'=4] {'tp'}, dimensions={0}, use_global_device_ids=true | all-gather | bytes 20480 | tf_op jit(solution)/shard_map/all_gather | solution.py:63
  297.1 1.3 fusion.32
  (35 shorter events, 1.5 us)
Async XLA Ops:
  7.2 59.9 %copy-start = (bf16[2048,768]{1,0:T(8,128)(2,1)S(1)}, bf16[2048,768]{1,0:T(8,128)(2,1)}, u32[]{:S(2)}) copy-start(bf16[2048,768]{1,0:T(8,128)(2,1)} %param.9) | copy-start | bytes 9437188
  7.2 59.9 %all-gather.13.cloned.1.call-start = ((), (), s32[]{:S(2)}) async-start(), calls=%async_computation.2 | async-start | bytes 8650752 | tf_op jit(solution)/shard_map/all_gather | solution.py:51
  11.4 110.5 %all-gather.15.cloned.1.call-start = ((), (), s32[]{:S(2)}) async-start(), calls=%async_computation.3 | async-start | bytes 8650752 | tf_op jit(solution)/shard_map/all_gather | solution.py:51
  12.1 164.5 %all-gather.17.cloned.1.call-start = ((), (), s32[]{:S(2)}) async-start(), calls=%async_computation.4 | async-start | bytes 8650752 | tf_op jit(solution)/shard_map/all_gather | solution.py:51
  12.9 223.4 %all-gather.11.cloned.1.call-start = ((), (), s32[]{:S(2)}) async-start(), calls=%async_computation.1 | async-start | bytes 10813440 | tf_op jit(solution)/shard_map/all_gather | solution.py:51
  271.3 13.3 %all-to-all-start = ((f32[4,32,256]{2,0,1:T(4,128)}), f32[4,32,256]{2,0,1:T(4,128)S(1)}, u32[]{:S(2)}, u32[]{:S(2)}) async-start(f32[4,32,256]{2,0,1:T(4,128)} %maximum_maximum_fusion), calls=%async_computation | async-start | bytes 262144 | tf_op jit(solution)/shard_map/all_to_all | solution.py:60
Sparse Core Ops, SparseCore 0:
  11.5 55.4 all-gather.12
  69.3 52.5 all-gather.14
  124.1 52.5 all-gather.16
  178.8 57.4 all-gather.10
where the time goes:
time: 307 us
  waiting for transfers between devices  198 us (64%)
  matrix products  43.3 us (14%)
  other arithmetic  19.3 us (6%)
  between operations  16.4 us (5%)
  blocking collectives  12.3 us (4%)
  local copies, waits for them, and re-layouts  12.1 us (4%)
  starting transfers between devices  5.6 us (2%)
    all_gather x4, waiting for transfers between devices, per_device(): block = lax.all_gather(piece, 'req', axis=0, tiled=False)  189 us
    dot_general x4, matrix products, chunk_stats(): logits = jnp.dot(block, matrix, preferred_element_type=jnp.float32)  43.3 us
    all_gather x1, blocking collectives, per_device(): everyone = lax.all_gather(own, 'tp', axis=0)  12.3 us
    reduce_sum x1, other arithmetic, chunk_stats(): weight_sum = jnp.sum(shifted, axis=-1)  12 us
    slice x1, local copies, waits for them, and re-layouts, per_device(): block = block[:, :step]  8.39 us
    all_to_all x1, waiting for transfers between devices, per_device(): lax.all_to_all(stats, 'req', split_axis=1, concat_axis=1, tiled=True)  7.21 us
  transfers between devices with their start and end apart: 5, of which 5 were waited for; matrix products, arithmetic and copies ran while one was open for 11% of the time, Pallas kernels for 0%

commit v1 on v0

--- a/solution.py
+++ b/solution.py
@@ -4,6 +4,12 @@
 from jax.sharding import PartitionSpec as P
 
 CHUNKS = 4
+
+
+def exchange_blocks(value, mesh_axis, split, join):
+    shards = jnp.split(value, lax.axis_size(mesh_axis), axis=split)
+    got = lax.all_to_all(jnp.stack(shards), mesh_axis, 0, 0)
+    return jnp.concatenate(got, axis=join)
 
 
 def chunk_stats(block, target, matrix, vocab_ids):
@@ -57,7 +63,7 @@
         st = chunk_stats(block.reshape(-1, block.shape[2]), target, head, own_vocab)
         parts.append(st.reshape(4, n_req, step))
     stats = jnp.concatenate(parts, axis=2)
-    arrived = lax.all_to_all(stats, "req", split_axis=1, concat_axis=1, tiled=True)
+    arrived = exchange_blocks(stats, "req", 1, 1)
     own = merge(jnp.moveaxis(arrived, 1, 0), axis=0)
     own = jnp.stack(own)
     everyone = lax.all_gather(own, "tp", axis=0)

time: 307 us -> 325 us (1.059)
  local copies, waits for them, and re-layouts: 12.1 us -> 31 us
    unnamed x3 -> x34, local copies, waits for them, and re-layouts: 0.01 us -> 18.3 us
  transfers between devices with their start and end apart: 5 -> 5, of which waited for: 5 -> 5; matrix products, arithmetic and copies ran while one was open for 11% -> 10% of each run, Pallas kernels for 0% -> 0%
where the time goes in v1:
time: 325 us
  waiting for transfers between devices  198 us (61%)
  matrix products  43.3 us (13%)
  local copies, waits for them, and re-layouts  31 us (10%)
  other arithmetic  18.7 us (6%)
  between operations  16.4 us (5%)
  blocking collectives  12.3 us (4%)
  starting transfers between devices  5.6 us (2%)
    all_gather x4, waiting for transfers between devices, per_device(): block = lax.all_gather(piece, 'req', axis=0, tiled=False)  189 us
    dot_general x4, matrix products, chunk_stats(): logits = jnp.dot(block, matrix, preferred_element_type=jnp.float32)  43.3 us
    unnamed x34, local copies, waits for them, and re-layouts  18.3 us
    all_gather x1, blocking collectives, per_device(): everyone = lax.all_gather(own, 'tp', axis=0)  12.3 us
    reduce_sum x1, other arithmetic, chunk_stats(): weight_sum = jnp.sum(shifted, axis=-1)  12 us
    slice x1, local copies, waits for them, and re-layouts, per_device(): block = block[:, :step]  8.39 us
    all_to_all x1, waiting for transfers between devices, exchange_blocks(): got = lax.all_to_all(jnp.stack(shards), mesh_axis, 0, 0)  7.21 us
  transfers between devices with their start and end apart: 5, of which 5 were waited for; matrix products, arithmetic and copies ran while one was open for 10% of the time, Pallas kernels for 0%

profile of v1, /device:TPU:0, one launch (start us, length us, event | category | flops | bytes accessed | tf_op | source)
XLA Modules:
  0.0 325.0 jit_solution(8526584782720007369)
XLA Ops:
  7.2 1.7 fusion.4
  8.9 1.5 fusion.6
  10.4 0.9 fusion.33
  11.4 0.7 all-gather.15.cloned.1.call-update
  12.2 0.7 all-gather.17.cloned.1.call-update
  12.9 0.7 fusion.29
  13.7 0.8 pad_maximum_fusion
  14.5 52.5 %all-gather.13.cloned.1.call-done = bf16[2048,2048]{1,0:T(8,128)(2,1)} async-done(((bf16[64,2048]{1,0:T(8,128)(2,1)}), bf16[2048,2048]{1,0:T(8,128)(2,1)}) %all-gather.13.cloned.1.call-update) | async-done | bytes 8388624 | tf_op jit(solution)/shard_map/all_gather | solution.py:57
  67.0 10.8 %fusion.38 = (f32[2048]{0:T(1024)S(1)}, f32[2048,768]{0,1:T(8,128)}) fusion(bf16[2048,2048]{1,0:T(8,128)(2,1)} %all-gather.13.cloned.1.call-done, bf16[2048,768]{1,0:T(8,128)(2,1)S(1)} %copy-done), kind=kOutput, calls=%fused_computation.156 | convolution fusion | flops 6444021760 | bytes 17833984 | tf_op jit(solution)/shard_map/dot_general | solution.py:16
  77.9 43.9 %all-gather.15.cloned.1.call-done = bf16[2048,2048]{1,0:T(8,128)(2,1)} async-done(((bf16[64,2048]{1,0:T(8,128)(2,1)}), bf16[2048,2048]{1,0:T(8,128)(2,1)}) %all-gather.15.cloned.1.call-update) | async-done | bytes 8388624 | tf_op jit(solution)/shard_map/all_gather | solution.py:57
  121.8 10.8 %fusion.39 = (f32[2048]{0:T(1024)S(1)}, f32[2048,768]{0,1:T(8,128)}) fusion(bf16[2048,2048]{1,0:T(8,128)(2,1)} %all-gather.15.cloned.1.call-done, bf16[2048,768]{1,0:T(8,128)(2,1)S(1)} %copy-done), kind=kOutput, calls=%fused_computation.157 | convolution fusion | flops 6444021760 | bytes 17833984 | tf_op jit(solution)/shard_map/dot_general | solution.py:16
  132.7 44.0 %all-gather.17.cloned.1.call-done = bf16[2048,2048]{1,0:T(8,128)(2,1)} async-done(((bf16[64,2048]{1,0:T(8,128)(2,1)}), bf16[2048,2048]{1,0:T(8,128)(2,1)}) %all-gather.17.cloned.1.call-update) | async-done | bytes 8388624 | tf_op jit(solution)/shard_map/all_gather | solution.py:57
  176.7 10.8 %fusion.40 = (f32[2048]{0:T(1024)S(1)}, f32[2048,768]{0,1:T(8,128)}) fusion(bf16[2048,2048]{1,0:T(8,128)(2,1)} %all-gather.17.cloned.1.call-done, bf16[2048,768]{1,0:T(8,128)(2,1)S(1)} %copy-done), kind=kOutput, calls=%fused_computation.158 | convolution fusion | flops 6444021760 | bytes 17833984 | tf_op jit(solution)/shard_map/dot_general | solution.py:16
  187.5 48.7 %all-gather.11.cloned.1.call-done = bf16[2560,2048]{1,0:T(8,128)(2,1)} async-done(((bf16[80,2048]{1,0:T(8,128)(2,1)}), bf16[2560,2048]{1,0:T(8,128)(2,1)}) %all-gather.11.cloned.1.call-update) | async-done | bytes 10485776 | tf_op jit(solution)/shard_map/all_gather | solution.py:57
  236.2 1.0 slice.104
  237.3 8.4 %slice.103 = bf16[32,64,2048]{2,1,0:T(8,128)(2,1)} slice(bf16[32,80,2048]{2,1,0:T(8,128)(2,1)} %bitcast.201), slice={[0:32], [0:64], [0:2048]} | slice | bytes 16777216 | tf_op jit(solution)/shard_map/slice | solution.py:61
  246.2 10.9 %fusion.37 = (f32[2048]{0:T(1024)S(1)}, f32[2048,768]{0,1:T(8,128)}) fusion(bf16[2048,2048]{1,0:T(8,128)(2,1)} %bitcast.199, bf16[2048,768]{1,0:T(8,128)(2,1)S(1)} %copy-done), kind=kOutput, calls=%fused_computation.155 | convolution fusion | flops 6444021760 | bytes 17833984 | tf_op jit(solution)/shard_map/dot_general | solution.py:16
  257.2 12.0 %fusion.3 = (f32[2048]{0:T(1024)S(1)}, f32[2048]{0:T(1024)S(1)}, f32[2048]{0:T(1024)S(1)}, f32[2048]{0:T(1024)S(1)}, f32[2048]{0:T(1024)S(1)}, /*index=5*/f32[20...) fusion(f32[2048,768]{0,1:T(8,128)} %get-tuple-element.71, ...), kind=kLoop, calls=%fused_computation.15 | loop fusion | flops 44015616 | bytes 25332736 | tf_op jit(solution)/shard_map/reduce_sum | solution.py:19
  270.6 0.6 constant_dynamic-update-slice_fusion.31
  271.2 0.6 constant_dynamic-update-slice_fusion.30
  274.2 0.6 constant_dynamic-update-slice_fusion.25
  276.5 0.6 constant_dynamic-update-slice_fusion.21
  278.3 0.6 constant_dynamic-update-slice_fusion.18
  281.3 0.6 constant_dynamic-update-slice_fusion.13
  281.9 0.6 constant_dynamic-update-slice_fusion.12
  283.1 0.6 constant_dynamic-update-slice_fusion.10
  284.8 0.6 constant_dynamic-update-slice_fusion.7
  286.0 0.6 constant_dynamic-update-slice_fusion.5
  289.6 5.4 %all-to-all-start = ((f32[32,4,1,256]{3,1,2,0:T(4,128)}), f32[32,4,1,256]{3,1,2,0:T(4,128)S(1)}, u32[]{:S(2)}, u32[]{:S(2)}) async-start(f32[32,4,1,256]{3,1,2,0:T(4,128)} %constant_dynamic-update-slice_fusion), calls=%async_computation | async-start | bytes 262144 | tf_op jit(solution)/shard_map/all_to_all | solution.py:11
  295.6 7.2 %all-to-all-done = f32[32,4,1,256]{3,1,2,0:T(4,128)S(1)} async-done(((f32[32,4,1,256]{3,1,2,0:T(4,128)}), f32[32,4,1,256]{3,1,2,0:T(4,128)S(1)}, u32[]{:S(2)}, u32[]{:S(2)}) %all-to-all-start) | async-done | bytes 131104 | tf_op jit(solution)/shard_map/all_to_all | solution.py:11
  303.0 12.3 %all-gather.5 = f32[4,4,256]{2,1,0:T(4,128)S(1)} all-gather(f32[1,4,256]{2,1,0:T(4,128)S(1)} %maximum_bitcast_fusion), channel_id=6, replica_groups=mesh['req'=32,'tp'=4] {'tp'}, dimensions={0}, use_global_device_ids=true | all-gather | bytes 20480 | tf_op jit(solution)/shard_map/all_gather | solution.py:69
  315.4 1.3 fusion.32
  (67 shorter events, 15.7 us)
Async XLA Ops:
  7.2 59.9 %copy-start = (bf16[2048,768]{1,0:T(8,128)(2,1)S(1)}, bf16[2048,768]{1,0:T(8,128)(2,1)}, u32[]{:S(2)}) copy-start(bf16[2048,768]{1,0:T(8,128)(2,1)} %param.9) | copy-start | bytes 9437188
  7.2 59.9 %all-gather.13.cloned.1.call-start = ((), (), s32[]{:S(2)}) async-start(), calls=%async_computation.2 | async-start | bytes 8650752 | tf_op jit(solution)/shard_map/all_gather | solution.py:57
  11.4 110.5 %all-gather.15.cloned.1.call-start = ((), (), s32[]{:S(2)}) async-start(), calls=%async_computation.3 | async-start | bytes 8650752 | tf_op jit(solution)/shard_map/all_gather | solution.py:57
  12.1 164.5 %all-gather.17.cloned.1.call-start = ((), (), s32[]{:S(2)}) async-start(), calls=%async_computation.4 | async-start | bytes 8650752 | tf_op jit(solution)/shard_map/all_gather | solution.py:57
  12.9 223.4 %all-gather.11.cloned.1.call-start = ((), (), s32[]{:S(2)}) async-start(), calls=%async_computation.1 | async-start | bytes 10813440 | tf_op jit(solution)/shard_map/all_gather | solution.py:57
  289.6 13.3 %all-to-all-start = ((f32[32,4,1,256]{3,1,2,0:T(4,128)}), f32[32,4,1,256]{3,1,2,0:T(4,128)S(1)}, u32[]{:S(2)}, u32[]{:S(2)}) async-start(f32[32,4,1,256]{3,1,2,0:T(4,128)} %constant_dynamic-update-slice_fusion), calls=%async_computation | async-start | bytes 262144 | tf_op jit(solution)/shard_map/all_to_all | solution.py:11
Sparse Core Ops, SparseCore 0:
  11.5 55.4 all-gather.12
  69.3 52.5 all-gather.14
  124.1 52.5 all-gather.16
  178.8 57.4 all-gather.10
